TPU v7x, 128 devices: a whole 4x4x4 slice. The times are simulated.
128 devices in a mesh: grp: 4 (over z), tok: 32 (over y, x, core).
Axes of the slice: x: 4, y: 4, z: 4, core: 2. Of those that a mesh axis runs over, the one named last changes fastest.
Arguments:
- tokens: bfloat16 [32768, 1408], P(('grp', 'tok')), may hold values from -6 to 6
- seg_ids: int32 [32768], P(('grp', 'tok')), may hold values from 0 to 8191, as said below
- merge_index: int32 [32768], P(('grp', 'tok')), may hold values from 0 to 255, as said below
- owners: int32 [8192, 1], P(('grp', 'tok')), may hold values from 0 to 31; in each aligned block of 64 rows (0 to 63, 64 to 127, ...) at most 4 rows name the same one
- w_qkv: bfloat16 [1408, 2112], replicated, may hold values from -0.15625 to 0.15625
- w_attn_out: bfloat16 [704, 1408], replicated, may hold values from -1.75 to 1.75
- w_in: bfloat16 [6144, 1408], P('grp'), may hold values from -0.15625 to 0.15625
- in_bias: bfloat16 [6144], P('grp'), may hold values from -3 to 3
- w_out: bfloat16 [6144, 1408], P('grp'), may hold values from -0.078125 to 0.078125
- out_bias: float32 [1408], replicated, may hold values from -3 to 3
- merge_gain: float32 [1408], replicated, may hold values from 0.1 to 1.9
- w_merge: bfloat16 [5632, 2048], P(None, 'grp'), may hold values from -0.078125 to 0.078125
- merge_bias: float32 [2048], P('grp'), may hold values from -3 to 3
Outputs:
- embeds: bfloat16 [16384, 2048], P('tok', 'grp')
Inputs may be any that keep to these rules, and one draw needn't show every extreme that they name: `seg_ids`: never falling along the tokens; every segment starts at a multiple of 4 tokens, has a multiple of 4 tokens and lies within one aligned block of 8192 tokens. `merge_index`: in each aligned block of 256 entries the values are a permutation of 0 to 255, and each aligned group of 4 entries names rows of a single segment. `owners`: among the 64 merged tokens of one device no owner is named more than 4 times.
All inputs are finite; a program needn't handle non-finite values.
Results may differ from a plain program's by a relative error of at most 0.014.
Values may be sent and summed in bfloat16 or wider, within the bound.
No kernel may reach another device: no remote copies, remote signals or barrier semaphores. Data moves between devices by JAX's collectives and lax.ppermute only.
A program may use at most 320 MiB of HBM per device.

v0:
```python
import math
import jax
import jax.numpy as jnp
from jax import lax
from jax.sharding import PartitionSpec as P

HEADS = 8
HD = 88
NORM_EPS = 1e-06


def layer_norm(values):
    centred = values - jnp.mean(values, axis=-1, keepdims=True)
    return centred * lax.rsqrt(jnp.mean(centred * centred, axis=-1, keepdims=True) + NORM_EPS)


def head_norm(values):
    return values * lax.rsqrt(jnp.mean(values * values, axis=-1, keepdims=True) + NORM_EPS)


def local(
    tokens,
    seg_ids,
    merge_index,
    owners,
    w_qkv,
    w_attn_out,
    w_in,
    in_bias,
    w_out,
    out_bias,
    merge_gain,
    w_merge,
    merge_bias,
):
    tok_rows = tokens.shape[0]
    feat_width = tokens.shape[1]
    head_width = HEADS * HD
    normed = layer_norm(tokens.astype(jnp.float32)).astype(jnp.bfloat16)
    projected = jnp.dot(normed, w_qkv, preferred_element_type=jnp.float32).astype(jnp.bfloat16)
    queries = head_norm(
        projected[:, :head_width].astype(jnp.float32).reshape(tok_rows, HEADS, HD)
    ).astype(jnp.bfloat16)
    key_rows = head_norm(
        projected[:, head_width : 2 * head_width].astype(jnp.float32).reshape(tok_rows, HEADS, HD)
    ).astype(jnp.bfloat16)
    keys_values = jnp.concatenate(
        [key_rows.reshape(tok_rows, head_width), projected[:, 2 * head_width :]], axis=1
    )
    score_scale = 1.0 / math.sqrt(HD)
    piece_kv = lax.all_gather(keys_values, "tok", axis=0, tiled=True)
    piece_seg = lax.all_gather(seg_ids, "tok", axis=0, tiled=True)
    row_count = piece_kv.shape[0]
    piece_keys = piece_kv[:, :head_width].reshape(row_count, HEADS, HD)
    piece_values = piece_kv[:, head_width:].reshape(row_count, HEADS, HD)
    scores = (
        jnp.einsum("qhd,khd->hqk", queries, piece_keys, preferred_element_type=jnp.float32)
        * score_scale
    )
    same_segment = (seg_ids[:, None] == piece_seg[None, :])[None]
    weights = jnp.where(same_segment, jnp.exp(scores), 0.0)
    denominator = jnp.sum(weights, axis=-1)
    numerator = jnp.einsum(
        "hqk,khd->qhd",
        weights.astype(jnp.bfloat16),
        piece_values,
        preferred_element_type=jnp.float32,
    )
    numerator, denominator = (numerator, denominator)
    attended = (
        (numerator / jnp.transpose(denominator)[:, :, None])
        .astype(jnp.bfloat16)
        .reshape(tok_rows, head_width)
    )
    residual = (
        tokens.astype(jnp.float32)
        + jnp.dot(attended, w_attn_out, preferred_element_type=jnp.float32)
    ).astype(jnp.bfloat16)
    mlp_in = layer_norm(residual.astype(jnp.float32)).astype(jnp.bfloat16)
    pre_act = lax.dot_general(
        lax.all_gather(mlp_in, "grp", axis=0, tiled=True),
        w_in,
        (((1,), (1,)), ((), ())),
        preferred_element_type=jnp.float32,
    )
    hidden = jax.nn.gelu(pre_act + in_bias.astype(jnp.float32), approximate=False).astype(
        jnp.bfloat16
    )
    mlp_sum = lax.psum_scatter(
        jnp.dot(hidden, w_out, preferred_element_type=jnp.float32).astype(jnp.bfloat16),
        "grp",
        scatter_dimension=0,
        tiled=True,
    ).astype(jnp.float32)
    normed_out = (
        layer_norm(residual.astype(jnp.float32) + mlp_sum + out_bias) * merge_gain
    ).astype(jnp.bfloat16)
    merged_count = tok_rows // 4
    merged = jnp.take(normed_out, merge_index, axis=0).reshape(merged_count, 4 * feat_width)
    tok_devices = lax.axis_size("tok")
    grp_devices = lax.axis_size("grp")
    slot_cap = max(2, 2 * merged_count // tok_devices)
    owner_col = owners[:, 0]
    positions = jnp.arange(merged_count, dtype=jnp.int32)
    earlier = (owner_col[:, None] == owner_col[None, :]) & (positions[None, :] < positions[:, None])
    owner_rank = jnp.sum(earlier.astype(jnp.int32), axis=1)
    slot_index = owner_col * slot_cap + owner_rank
    merged_all, slots_all = (
        lax.all_gather(merged, "grp", axis=0, tiled=True),
        lax.all_gather(slot_index, "grp", axis=0, tiled=True),
    )
    embedded = (
        jnp.dot(merged_all, w_merge, preferred_element_type=jnp.float32) + merge_bias
    ).astype(jnp.bfloat16)
    out_cols = embedded.shape[1]
    slot_range = jnp.arange(tok_devices * slot_cap, dtype=jnp.int32)
    placement = (
        slots_all.reshape(grp_devices, 1, merged_count) == slot_range[None, :, None]
    ).astype(jnp.bfloat16)
    placement = placement.reshape(grp_devices, tok_devices, slot_cap, merged_count)
    outgoing = jnp.einsum(
        "gjrm,gmc->jgrc",
        placement,
        embedded.reshape(grp_devices, merged_count, out_cols),
        preferred_element_type=jnp.float32,
    ).astype(jnp.bfloat16)
    received = lax.all_to_all(outgoing, "tok", split_axis=0, concat_axis=2, tiled=True)
    return received.reshape(grp_devices * tok_devices * slot_cap, out_cols)


def solution(mesh):
    placed = (
        P(("grp", "tok"), None),
        P(("grp", "tok")),
        P(("grp", "tok")),
        P(("grp", "tok"), None),
        P(),
        P(),
        P("grp", None),
        P("grp"),
        P("grp", None),
        P(),
        P(),
        P(None, "grp"),
        P("grp"),
    )
    return jax.shard_map(
        local, mesh=mesh, in_specs=placed, out_specs=P("tok", "grp"), check_vma=False
    )
```

profile of v0, /device:TPU:1, one launch (start us, length us, event | category | flops | bytes accessed | tf_op | source)
XLA Modules:
  0.0 376.1 jit_solution(4948535860461258292)
XLA Ops:
  6.5 1.4 convert_reduce_fusion
  8.0 1.4 fusion.21
  9.4 4.9 %convolution_convert_fusion = bf16[256,2112]{0,1:T(8,128)(2,1)S(1)} fusion(bf16[1408,2112]{0,1:T(8,128)(2,1)} %param.17, bf16[256,1408]{1,0:T(8,128)(2,1)} %param.13, f32[256]{0:T(256)S(1)} %add_rsqrt_fusion.4, f32[256]{0:T(256)S(1)} %broadcast_multiply_fusion.2), kind=kOutput, calls=%fused_computation.28 | convolution fusion | flops 1524514816 | bytes 7751680 | tf_op jit(solution)/shard_map/dot_general | solution.py:40
  14.4 0.1 convert_multiply_fusion.3
  14.4 0.9 copy-done.2
  15.4 0.1 reduce_sum.92
  15.5 1.1 fusion.34
  16.5 0.9 pad_maximum_fusion
  17.4 0.0 all-gather.5.cloned.1.call-update
  17.5 0.0 all-gather.7.cloned.1.call-start
  17.5 26.0 %all-gather = s32[32,1,256]{2,1,0:T(1,128)S(1)} all-gather(s32[1,1,256]{2,1,0:T(1,128)S(1)} %bitcast.54), channel_id=1, replica_groups=mesh['grp'=4,'tok'=32] {'tok'}, dimensions={0}, use_global_device_ids=true | all-gather | bytes 33792 | tf_op jit(solution)/shard_map/all_gather | solution.py:52
  43.5 0.1 fusion.35
  43.6 2.5 broadcast_compare_fusion
  46.1 72.6 %all-gather.5.cloned.1.call-done = bf16[8192,1408]{0,1:T(8,128)(2,1)} async-done(((bf16[256,1408]{0,1:T(8,128)(2,1)}), bf16[8192,1408]{0,1:T(8,128)(2,1)}) %all-gather.5.cloned.1.call-update) | async-done | bytes 23068688 | tf_op jit(solution)/shard_map/all_gather | solution.py:51
  118.7 16.6 %fusion.80 = (bf16[8192,704]{0,1:T(8,128)(2,1)}, bf16[8192,704]{0,1:T(8,128)(2,1)}) fusion(bf16[8192,1408]{0,1:T(8,128)(2,1)} %all-gather.5.cloned.1.call-done), kind=kLoop, calls=%fused_computation.116 | loop fusion | bytes 46137344 | tf_op jit(solution)/shard_map/slice | solution.py:54
  135.3 32.1 %fusion = (f32[8,256]{1,0:T(8,128)S(1)}, f32[8,256,8192]{2,1,0:T(8,128)}) fusion(pred[256,8192]{1,0:T(8,128)(4,1)} %broadcast_compare_fusion, bf16[8192,8,88]{0,2,1:T(8,128)(2,1)} %bitcast.44, bf16[256,8,88]{0,2,1:T(8,128)(2,1)S(1)} %bitcast.50, f32[256,8]{0,1:T(8,128)S(1)} %add_rsqrt_fusion), kind=kOutput, calls=%fused_computation.2 | convolution fusion | flops 3003660288 | bytes 81117184 | tf_op jit(solution)/shard_map/qhd,khd->hqk/dot_general | solution.py:57
  167.4 28.2 %fusion.30 = bf16[256,8,88]{0,2,1:T(8,128)(2,1)} fusion(bf16[8192,8,88]{0,2,1:T(8,128)(2,1)} %bitcast.43, f32[8,256,8192]{2,1,0:T(8,128)} %get-tuple-element.10, pred[256,8192]{1,0:T(8,128)(4,1)} %broadcast_compare_fusion, f32[256,8]{0,1:T(8,128)S(1)} %bitcast.56), kind=kOutput, calls=%fused_computation.48 | convolution fusion | flops 3003482112 | bytes 81108992 | tf_op jit(solution)/shard_map/hqk,khd->qhd/dot_general | solution.py:63
  195.6 2.1 fusion.82
  197.7 0.3 multiply_reduce_fusion.1
  198.0 1.1 multiply_convert_fusion.1
  199.1 0.0 all-gather.7.cloned.1.call-update
  199.2 0.3 reduce-scatter.2.cloned.1.call-start
  199.5 37.7 %all-gather.7.cloned.1.call-done = bf16[1024,1408]{1,0:T(8,128)(2,1)} async-done(((bf16[256,1408]{1,0:T(8,128)(2,1)}), bf16[1024,1408]{1,0:T(8,128)(2,1)}) %all-gather.7.cloned.1.call-update) | async-done | bytes 2883600 | tf_op jit(solution)/shard_map/all_gather | solution.py:81
  237.2 25.3 %convolution_convert_fusion.1 = bf16[1024,1408]{1,0:T(8,128)(2,1)} fusion(bf16[1536,1408]{1,0:T(8,128)(2,1)} %param.21, bf16[1024,1408]{1,0:T(8,128)(2,1)} %all-gather.7.cloned.1.call-done, bf16[1536,1408]{1,0:T(8,128)(2,1)} %param.19, f32[1536]{0:T(1024)S(1)} %convert_element_type.76), kind=kOutput, calls=%fused_computation.29 | convolution fusion | flops 8963620864 | bytes 14424064 | tf_op jit(solution)/shard_map/dot_general | solution.py:90
  262.5 0.0 reduce-scatter.2.cloned.1.call-update
  262.6 0.3 all-gather.9.cloned.1.call-start
  262.9 0.1 broadcast_in_dim.25
  263.0 0.3 broadcast_in_dim.29
  263.3 0.2 copy.20
  263.5 35.6 %reduce-scatter.2.cloned.1.call-done = bf16[256,1408]{1,0:T(8,128)(2,1)} async-done(((bf16[1024,1408]{1,0:T(8,128)(2,1)}), bf16[256,1408]{1,0:T(8,128)(2,1)}) %reduce-scatter.2.cloned.1.call-update) | async-done | bytes 720912 | tf_op jit(solution)/shard_map/reduce_scatter | solution.py:89
  299.1 1.4 fusion.40
  300.5 1.5 multiply_reduce_fusion
  302.0 1.5 multiply_convert_fusion
  303.5 1.3 gather_fusion
  304.8 0.5 gather.7
  305.3 1.0 broadcast_select_fusion
  306.2 0.6 dynamic-slice
  307.5 0.2 convert_reduce_fusion.1
  307.7 0.1 add_dynamic-update-slice_fusion
  307.8 5.3 %all-reduce = s32[256]{0:T(256)S(1)} all-reduce(s32[256]{0:T(256)S(1)} %add_dynamic-update-slice_fusion), channel_id=1, replica_groups=mesh['grp'=4,'tok'=32] {'grp'}, use_global_device_ids=true, to_apply=%add | all-reduce | flops 256 | bytes 2048
  313.1 0.1 eq.58
  313.2 30.3 %all-gather.9.cloned.1.call-done = bf16[256,5632]{1,0:T(8,128)(2,1)} async-done(((bf16[64,5632]{1,0:T(8,128)(2,1)}), bf16[256,5632]{1,0:T(8,128)(2,1)}) %all-gather.9.cloned.1.call-update) | async-done | bytes 2883600 | tf_op jit(solution)/shard_map/all_gather | solution.py:109
  343.5 5.3 %fusion.33 = bf16[256,512]{1,0:T(8,128)(2,1)S(1)} fusion(bf16[256,5632]{1,0:T(8,128)(2,1)} %all-gather.9.cloned.1.call-done, bf16[5632,512]{1,0:T(8,128)(2,1)} %param.24, f32[512]{0:T(512)S(1)} %copy-done.9), kind=kOutput, calls=%fused_computation.50 | convolution fusion | flops 1476657152 | bytes 8914944 | tf_op jit(solution)/shard_map/dot_general | solution.py:113
  348.8 0.3 fusion.26
  349.2 0.4 copy.17
  349.6 18.9 %all_to_all.15 = bf16[32,4,4,512]{3,2,1,0:T(4,128)(2,1)S(1)} all-to-all(bf16[32,4,4,512]{3,2,1,0:T(4,128)(2,1)S(1)} %copy.17), channel_id=1, replica_groups=mesh['grp'=4,'tok'=32] {'tok'}, dimensions={0} | all-to-all | bytes 1048576 | tf_op jit(solution)/shard_map/all_to_all | solution.py:127
  368.5 0.2 copy.18
  368.7 0.9 reshape.131
  (38 shorter events, 0.2 us)
Async XLA Ops:
  6.5 189.1 %copy-start = (bf16[704,1408]{1,0:T(8,128)(2,1)S(1)}, bf16[704,1408]{1,0:T(8,128)(2,1)}, u32[]{:S(2)}) copy-start(bf16[704,1408]{1,0:T(8,128)(2,1)} %param.18) | copy-start | bytes 5947396
  6.5 112.2 %all-gather.5.cloned.1.call-start = ((), (), s32[]{:S(2)}) async-start(), calls=%async_computation.2 | async-start | bytes 23789568 | tf_op jit(solution)/shard_map/all_gather | solution.py:51
  9.4 8.1 %copy-start.5 = (s32[256]{0:T(256)S(1)}, s32[256]{0:T(256)}, u32[]{:S(2)}) copy-start(s32[256]{0:T(256)} %param.14) | copy-start | bytes 3076
  14.3 1.0 copy-start.2
  17.5 219.8 %all-gather.7.cloned.1.call-start = ((), (), s32[]{:S(2)}) async-start(), calls=%async_computation.3 | async-start | bytes 3604480 | tf_op jit(solution)/shard_map/all_gather | solution.py:81
  195.6 3.8 %copy-start.6 = (bf16[1536]{0:T(1024)(128)(2,1)S(1)}, bf16[1536]{0:T(1024)(128)(2,1)}, u32[]{:S(2)}) copy-start(bf16[1536]{0:T(1024)(128)(2,1)} %param.20) | copy-start | bytes 9220
  199.2 99.9 %reduce-scatter.2.cloned.1.call-start = ((), (), s32[]{:S(2)}) async-start(), calls=%async_computation.4 | async-start | bytes 3604480 | tf_op jit(solution)/shard_map/reduce_scatter | solution.py:89
  199.5 63.4 %copy-start.7 = (s32[256]{0:T(256)S(1)}, s32[256]{0:T(256)}, u32[]{:S(2)}) copy-start(s32[256]{0:T(256)} %param.15) | copy-start | bytes 3076
  199.5 99.6 %copy-start.3 = (f32[1408]{0:T(1024)S(1)}, f32[1408]{0:T(1024)}, u32[]{:S(2)}) copy-start(f32[1408]{0:T(1024)} %param.22) | copy-start | bytes 16900
  262.5 39.4 %copy-start.4 = (f32[1408]{0:T(1024)S(1)}, f32[1408]{0:T(1024)}, u32[]{:S(2)}) copy-start(f32[1408]{0:T(1024)} %param.23) | copy-start | bytes 16900
  262.6 81.0 %all-gather.9.cloned.1.call-start = ((), (), s32[]{:S(2)}) async-start(), calls=%async_computation.5 | async-start | bytes 3604480 | tf_op jit(solution)/shard_map/all_gather | solution.py:109
  302.0 4.3 %copy-start.10 = (u32[128]{0:T(128)S(1)}, u32[128]{0:T(128)}, u32[]{:S(2)}) copy-start(u32[128]{0:T(128)} %constant.101) | copy-start | bytes 1540
  302.0 5.5 %copy-start.8 = (s32[64,1]{0,1:T(1,128)S(1)}, s32[64,1]{0,1:T(1,128)}, u32[]{:S(2)}) copy-start(s32[64,1]{0,1:T(1,128)} %param.16) | copy-start | bytes 772
  302.0 41.5 %copy-start.9 = (f32[512]{0:T(512)S(1)}, f32[512]{0:T(512)}, u32[]{:S(2)}) copy-start(f32[512]{0:T(512)} %param.25) | copy-start | bytes 6148
  343.5 26.1 %copy-start.1 = (bf16[704,1408]{1,0:T(8,128)(2,1)S(1)}, bf16[704,1408]{1,0:T(8,128)(2,1)}, u32[]{:S(2)}) copy-start(bf16[704,1408]{1,0:T(8,128)(2,1)} %param.18) | copy-start | bytes 5947396
Sparse Core Ops, SparseCore 0:
  17.6 101.0 all-gather.4
  199.3 37.8 all-gather.6
  262.7 36.3 reduce-scatter.1
  306.3 37.1 all-gather.8
where the time goes:
time: 377 us; the launch traced here: 376 us
  waiting for transfers between devices  176 us (47%)
  matrix products  98.3 us (26%)
  blocking collectives  50.2 us (13%)
  local copies, waits for them, and re-layouts  22.1 us (6%)
  other arithmetic  14.6 us (4%)
  between operations  14.1 us (4%)
    all_gather x1, waiting for transfers between devices, local(): piece_kv = lax.all_gather(keys_values, 'tok', axis=0, tiled=True)  72.6 us
    all_gather x1, waiting for transfers between devices, local(): lax.all_gather(mlp_in, 'grp', axis=0, tiled=True)  37.7 us
    reduce_scatter x1, waiting for transfers between devices, local(): lax.psum_scatter(jnp.dot(hidden, w_out, preferred_element_type=jnp.float3...  35.6 us
    dot_general x1, matrix products, local(): jnp.einsum('qhd,khd->hqk', queries, piece_keys, preferred_element_type=jn...  32.1 us
    all_gather x1, waiting for transfers between devices, local(): lax.all_gather(merged, 'grp', axis=0, tiled=True)  30.3 us
    dot_general x1, matrix products, local(): jnp.einsum('hqk,khd->qhd', weights.astype(jnp.bfloat16), piece_values, pr...  28.2 us
    all_gather x1, blocking collectives, local(): piece_seg = lax.all_gather(seg_ids, 'tok', axis=0, tiled=True)  26 us
    dot_general x1, matrix products, local(): jnp.dot(hidden, w_out, preferred_element_type=jnp.float32)  25.3 us
  transfers between devices with their start and end apart: 4, of which 4 were waited for; matrix products, arithmetic and copies ran while one was open for 1% of the time, Pallas kernels for 0%

commit v1 on v0

--- a/solution.py
+++ b/solution.py
@@ -124,7 +124,10 @@
         embedded.reshape(grp_devices, merged_count, out_cols),
         preferred_element_type=jnp.float32,
     ).astype(jnp.bfloat16)
-    received = lax.all_to_all(outgoing, "tok", split_axis=0, concat_axis=2, tiled=True)
+    size = lax.axis_size("tok")
+    blocks = jnp.stack(jnp.split(outgoing, size, axis=0), axis=0)
+    blocks = lax.all_to_all(blocks, "tok", split_axis=0, concat_axis=0)
+    received = jnp.concatenate(blocks, axis=2)
     return received.reshape(grp_devices * tok_devices * slot_cap, out_cols)
 
 

time: 377 us -> 378 us (level)
  no operation moved by 1% of the time
where the time goes in v1:
time: 378 us; the launch traced here: 377 us
  waiting for transfers between devices  176 us (47%)
  matrix products  98.3 us (26%)
  blocking collectives  50.2 us (13%)
  local copies, waits for them, and re-layouts  23.3 us (6%)
  other arithmetic  14.6 us (4%)
  between operations  14.2 us (4%)
    all_gather x1, waiting for transfers between devices, local(): piece_kv = lax.all_gather(keys_values, 'tok', axis=0, tiled=True)  72.6 us
    all_gather x1, waiting for transfers between devices, local(): lax.all_gather(mlp_in, 'grp', axis=0, tiled=True)  37.7 us
    reduce_scatter x1, waiting for transfers between devices, local(): lax.psum_scatter(jnp.dot(hidden, w_out, preferred_element_type=jnp.float3...  35.6 us
    dot_general x1, matrix products, local(): jnp.einsum('qhd,khd->hqk', queries, piece_keys, preferred_element_type=jn...  32.1 us
    all_gather x1, waiting for transfers between devices, local(): lax.all_gather(merged, 'grp', axis=0, tiled=True)  30.3 us
    dot_general x1, matrix products, local(): jnp.einsum('hqk,khd->qhd', weights.astype(jnp.bfloat16), piece_values, pr...  28.2 us
    all_gather x1, blocking collectives, local(): piece_seg = lax.all_gather(seg_ids, 'tok', axis=0, tiled=True)  26 us
    dot_general x1, matrix products, local(): jnp.dot(hidden, w_out, preferred_element_type=jnp.float32)  25.3 us
  transfers between devices with their start and end apart: 4, of which 4 were waited for; matrix products, arithmetic and copies ran while one was open for 1% of the time, Pallas kernels for 0%

profile of v1, /device:TPU:1, one launch (start us, length us, event | category | flops | bytes accessed | tf_op | source)
XLA Modules:
  0.0 377.5 jit_solution(7121965196488820097)
XLA Ops:
  6.5 1.4 convert_reduce_fusion
  8.0 1.4 fusion.21
  9.4 4.9 %convolution_convert_fusion = bf16[256,2112]{0,1:T(8,128)(2,1)S(1)} fusion(bf16[1408,2112]{0,1:T(8,128)(2,1)} %param.17, bf16[256,1408]{1,0:T(8,128)(2,1)} %param.13, f32[256]{0:T(256)S(1)} %add_rsqrt_fusion.4, f32[256]{0:T(256)S(1)} %broadcast_multiply_fusion.2), kind=kOutput, calls=%fused_computation.28 | convolution fusion | flops 1524514816 | bytes 7751680 | tf_op jit(solution)/shard_map/dot_general | solution.py:40
  14.4 0.1 convert_multiply_fusion.3
  14.4 0.9 copy-done.2
  15.4 0.1 reduce_sum.92
  15.5 1.1 fusion.34
  16.5 0.9 pad_maximum_fusion
  17.4 0.0 all-gather.5.cloned.1.call-update
  17.5 0.0 all-gather.7.cloned.1.call-start
  17.5 26.0 %all-gather = s32[32,1,256]{2,1,0:T(1,128)S(1)} all-gather(s32[1,1,256]{2,1,0:T(1,128)S(1)} %bitcast.116), channel_id=1, replica_groups=mesh['grp'=4,'tok'=32] {'tok'}, dimensions={0}, use_global_device_ids=true | all-gather | bytes 33792 | tf_op jit(solution)/shard_map/all_gather | solution.py:52
  43.5 0.1 fusion.35
  43.6 2.5 broadcast_compare_fusion
  46.1 72.6 %all-gather.5.cloned.1.call-done = bf16[8192,1408]{0,1:T(8,128)(2,1)} async-done(((bf16[256,1408]{0,1:T(8,128)(2,1)}), bf16[8192,1408]{0,1:T(8,128)(2,1)}) %all-gather.5.cloned.1.call-update) | async-done | bytes 23068688 | tf_op jit(solution)/shard_map/all_gather | solution.py:51
  118.7 16.6 %fusion.80 = (bf16[8192,704]{0,1:T(8,128)(2,1)}, bf16[8192,704]{0,1:T(8,128)(2,1)}) fusion(bf16[8192,1408]{0,1:T(8,128)(2,1)} %all-gather.5.cloned.1.call-done), kind=kLoop, calls=%fused_computation.148 | loop fusion | bytes 46137344 | tf_op jit(solution)/shard_map/slice | solution.py:54
  135.3 32.1 %fusion = (f32[8,256]{1,0:T(8,128)S(1)}, f32[8,256,8192]{2,1,0:T(8,128)}) fusion(pred[256,8192]{1,0:T(8,128)(4,1)} %broadcast_compare_fusion, bf16[8192,8,88]{0,2,1:T(8,128)(2,1)} %bitcast.106, bf16[256,8,88]{0,2,1:T(8,128)(2,1)S(1)} %bitcast.112, f32[256,8]{0,1:T(8,128)S(1)} %add_rsqrt_fusion), kind=kOutput, calls=%fused_computation.2 | convolution fusion | flops 3003660288 | bytes 81117184 | tf_op jit(solution)/shard_map/qhd,khd->hqk/dot_general | solution.py:57
  167.4 28.2 %fusion.30 = bf16[256,8,88]{0,2,1:T(8,128)(2,1)} fusion(bf16[8192,8,88]{0,2,1:T(8,128)(2,1)} %bitcast.105, f32[8,256,8192]{2,1,0:T(8,128)} %get-tuple-element.42, pred[256,8192]{1,0:T(8,128)(4,1)} %broadcast_compare_fusion, f32[256,8]{0,1:T(8,128)S(1)} %bitcast.118), kind=kOutput, calls=%fused_computation.48 | convolution fusion | flops 3003482112 | bytes 81108992 | tf_op jit(solution)/shard_map/hqk,khd->qhd/dot_general | solution.py:63
  195.6 2.1 fusion.84
  197.7 0.3 multiply_reduce_fusion.1
  198.0 1.1 multiply_convert_fusion.1
  199.1 0.0 all-gather.7.cloned.1.call-update
  199.2 0.3 reduce-scatter.2.cloned.1.call-start
  199.5 37.7 %all-gather.7.cloned.1.call-done = bf16[1024,1408]{1,0:T(8,128)(2,1)} async-done(((bf16[256,1408]{1,0:T(8,128)(2,1)}), bf16[1024,1408]{1,0:T(8,128)(2,1)}) %all-gather.7.cloned.1.call-update) | async-done | bytes 2883600 | tf_op jit(solution)/shard_map/all_gather | solution.py:81
  237.2 25.3 %convolution_convert_fusion.1 = bf16[1024,1408]{1,0:T(8,128)(2,1)} fusion(bf16[1536,1408]{1,0:T(8,128)(2,1)} %param.21, bf16[1024,1408]{1,0:T(8,128)(2,1)} %all-gather.7.cloned.1.call-done, bf16[1536,1408]{1,0:T(8,128)(2,1)} %param.19, f32[1536]{0:T(1024)S(1)} %convert_element_type.76), kind=kOutput, calls=%fused_computation.29 | convolution fusion | flops 8963620864 | bytes 14424064 | tf_op jit(solution)/shard_map/dot_general | solution.py:90
  262.6 0.3 all-gather.9.cloned.1.call-start
  262.9 0.1 broadcast_in_dim.25
  263.0 0.3 broadcast_in_dim.29
  263.3 0.2 copy.576
  263.5 35.6 %reduce-scatter.2.cloned.1.call-done = bf16[256,1408]{1,0:T(8,128)(2,1)} async-done(((bf16[1024,1408]{1,0:T(8,128)(2,1)}), bf16[256,1408]{1,0:T(8,128)(2,1)}) %reduce-scatter.2.cloned.1.call-update) | async-done | bytes 720912 | tf_op jit(solution)/shard_map/reduce_scatter | solution.py:89
  299.1 1.4 fusion.40
  300.5 1.5 multiply_reduce_fusion
  302.0 1.5 multiply_convert_fusion
  303.5 1.3 gather_fusion
  304.8 0.5 gather.7
  305.3 1.0 broadcast_select_fusion
  306.2 0.6 dynamic-slice
  307.5 0.2 convert_reduce_fusion.1
  307.7 0.1 add_dynamic-update-slice_fusion
  307.8 5.3 %all-reduce = s32[256]{0:T(256)S(1)} all-reduce(s32[256]{0:T(256)S(1)} %add_dynamic-update-slice_fusion), channel_id=1, replica_groups=mesh['grp'=4,'tok'=32] {'grp'}, use_global_device_ids=true, to_apply=%add | all-reduce | flops 256 | bytes 2048
  313.1 0.1 eq.58
  313.2 30.3 %all-gather.9.cloned.1.call-done = bf16[256,5632]{1,0:T(8,128)(2,1)} async-done(((bf16[64,5632]{1,0:T(8,128)(2,1)}), bf16[256,5632]{1,0:T(8,128)(2,1)}) %all-gather.9.cloned.1.call-update) | async-done | bytes 2883600 | tf_op jit(solution)/shard_map/all_gather | solution.py:109
  343.5 5.3 %fusion.33 = bf16[256,512]{1,0:T(8,128)(2,1)S(1)} fusion(bf16[256,5632]{1,0:T(8,128)(2,1)} %all-gather.9.cloned.1.call-done, bf16[5632,512]{1,0:T(8,128)(2,1)} %param.24, f32[512]{0:T(512)S(1)} %copy-done.9), kind=kOutput, calls=%fused_computation.50 | convolution fusion | flops 1476657152 | bytes 8914944 | tf_op jit(solution)/shard_map/dot_general | solution.py:113
  348.8 0.3 fusion.26
  349.2 0.4 fusion.83
  349.6 0.7 fusion.82
  351.0 18.9 %all_to_all.5 = bf16[32,1,4,4,512]{4,3,2,1,0:T(4,128)(2,1)S(1)} all-to-all(bf16[32,1,4,4,512]{4,3,2,1,0:T(4,128)(2,1)S(1)} %constant_dynamic-update-slice_fusion), channel_id=1, replica_groups=mesh['grp'=4,'tok'=32] {'tok'}, dimensions={0} | all-to-all | bytes 1048576 | tf_op jit(solution)/shard_map/all_to_all | solution.py:129
  369.8 0.2 copy.542
  370.0 0.9 reshape_reshape.3
  (71 shorter events, 0.8 us)
Async XLA Ops:
  6.5 189.1 %copy-start = (bf16[704,1408]{1,0:T(8,128)(2,1)S(1)}, bf16[704,1408]{1,0:T(8,128)(2,1)}, u32[]{:S(2)}) copy-start(bf16[704,1408]{1,0:T(8,128)(2,1)} %param.18) | copy-start | bytes 5947396
  6.5 112.2 %all-gather.5.cloned.1.call-start = ((), (), s32[]{:S(2)}) async-start(), calls=%async_computation.2 | async-start | bytes 23789568 | tf_op jit(solution)/shard_map/all_gather | solution.py:51
  9.4 8.1 %copy-start.5 = (s32[256]{0:T(256)S(1)}, s32[256]{0:T(256)}, u32[]{:S(2)}) copy-start(s32[256]{0:T(256)} %param.14) | copy-start | bytes 3076
  14.3 1.0 copy-start.2
  17.5 219.8 %all-gather.7.cloned.1.call-start = ((), (), s32[]{:S(2)}) async-start(), calls=%async_computation.3 | async-start | bytes 3604480 | tf_op jit(solution)/shard_map/all_gather | solution.py:81
  195.6 3.8 %copy-start.6 = (bf16[1536]{0:T(1024)(128)(2,1)S(1)}, bf16[1536]{0:T(1024)(128)(2,1)}, u32[]{:S(2)}) copy-start(bf16[1536]{0:T(1024)(128)(2,1)} %param.20) | copy-start | bytes 9220
  199.2 99.9 %reduce-scatter.2.cloned.1.call-start = ((), (), s32[]{:S(2)}) async-start(), calls=%async_computation.4 | async-start | bytes 3604480 | tf_op jit(solution)/shard_map/reduce_scatter | solution.py:89
  199.5 63.4 %copy-start.7 = (s32[256]{0:T(256)S(1)}, s32[256]{0:T(256)}, u32[]{:S(2)}) copy-start(s32[256]{0:T(256)} %param.15) | copy-start | bytes 3076
  199.5 99.6 %copy-start.3 = (f32[1408]{0:T(1024)S(1)}, f32[1408]{0:T(1024)}, u32[]{:S(2)}) copy-start(f32[1408]{0:T(1024)} %param.22) | copy-start | bytes 16900
  262.5 39.4 %copy-start.4 = (f32[1408]{0:T(1024)S(1)}, f32[1408]{0:T(1024)}, u32[]{:S(2)}) copy-start(f32[1408]{0:T(1024)} %param.23) | copy-start | bytes 16900
  262.6 81.0 %all-gather.9.cloned.1.call-start = ((), (), s32[]{:S(2)}) async-start(), calls=%async_computation.5 | async-start | bytes 3604480 | tf_op jit(solution)/shard_map/all_gather | solution.py:109
  302.0 4.3 %copy-start.10 = (u32[128]{0:T(128)S(1)}, u32[128]{0:T(128)}, u32[]{:S(2)}) copy-start(u32[128]{0:T(128)} %constant.101) | copy-start | bytes 1540
  302.0 5.5 %copy-start.8 = (s32[64,1]{0,1:T(1,128)S(1)}, s32[64,1]{0,1:T(1,128)}, u32[]{:S(2)}) copy-start(s32[64,1]{0,1:T(1,128)} %param.16) | copy-start | bytes 772
  302.0 41.5 %copy-start.9 = (f32[512]{0:T(512)S(1)}, f32[512]{0:T(512)}, u32[]{:S(2)}) copy-start(f32[512]{0:T(512)} %param.25) | copy-start | bytes 6148
  343.5 27.4 %copy-start.1 = (bf16[704,1408]{1,0:T(8,128)(2,1)S(1)}, bf16[704,1408]{1,0:T(8,128)(2,1)}, u32[]{:S(2)}) copy-start(bf16[704,1408]{1,0:T(8,128)(2,1)} %param.18) | copy-start | bytes 5947396
Sparse Core Ops, SparseCore 0:
  17.6 101.0 all-gather.4
  199.3 37.8 all-gather.6
  262.7 36.3 reduce-scatter.1
  306.3 37.1 all-gather.8
